TPU v7x, 256 devices: a whole 4x4x8 slice. The times are simulated.
256 devices in a mesh: gx: 32 (over y, z), gy: 8 (over x, core).
Axes of the slice: x: 4, y: 4, z: 8, core: 2. Of those that a mesh axis runs over, the one named last changes fastest.
Arguments:
- features: bfloat16 [2048, 64, 512], P(('gx', 'gy')), may hold values from -6 to 6
- neighbours: int32 [2048, 6], P(('gx', 'gy')), may hold values from 0 to 16, as said below
- counts: int32 [256], P(('gx', 'gy')), may hold values from 1 to 8, as said below
- conv_weight: bfloat16 [64, 448], replicated, may hold values from -0.25 to 0.25
- down_weight: bfloat16 [128, 512], replicated, may hold values from -0.25 to 0.25
- head_weight: bfloat16 [128, 128], replicated, may hold values from -0.5 to 0.5
- coarse_map: int32 [256, 8], P(('gx', 'gy')), may hold values from 0 to 32, as said below
- latent_grad: bfloat16 [256, 512, 128], P(('gx', 'gy')), may hold values from -6 to 6
Outputs:
- latent: bfloat16 [256, 512, 128], P(('gx', 'gy'))
- features_grad: bfloat16 [2048, 64, 512], P(('gx', 'gy'))
- conv_grad: float32 [64, 448], replicated
- down_grad: float32 [128, 512], replicated
- head_grad: float32 [128, 128], replicated
Inputs may be any that keep to these rules, and one draw needn't show every extreme that they name: `counts`: in every draw, max(1, (devices along gx times devices along gy) // 8) columns have exactly 8 active blocks; each other column has between 1 and 4. 16 means no neighbour; a value below 8 is an active slot of the same column; a value v of 8 or more is the active slot v - 8 of the adjacent column in that direction; the z directions never name another column; inactive slots have no neighbours. `coarse_map`: 32 marks an empty octant; every other entry names an active block's octant, and each such octant is named at most once among the four columns that share a merged list.
All inputs are finite; a program needn't handle non-finite values.
Results may differ from a plain program's by a relative error of at most 0.013.
Values may be sent and summed in bfloat16 or wider, within the bound.
A program may use at most 128 MiB of HBM per device.

v0:
```python
import jax
import jax.numpy as jnp
from jax import lax
from jax.sharding import PartitionSpec as P


def from_partner(block, axis, distance):
    count = lax.axis_size(axis)
    route = []
    for low in range(count):
        high = low | 1 << distance
        if high != low and high < count:
            route += [(low, high), (high, low)]
    return lax.ppermute(block, axis, route)


def padded(block, sides, width):
    for axis, dim in sides:
        count = lax.axis_size(axis)
        forward = [(i, i + 1) for i in range(count - 1)]
        backward = [(target, source) for source, target in forward]
        low = lax.ppermute(
            lax.slice_in_dim(block, block.shape[dim] - width, None, axis=dim), axis, forward
        )
        high = lax.ppermute(lax.slice_in_dim(block, 0, width, axis=dim), axis, backward)
        block = jnp.concatenate([low, block, high], axis=dim)
    return block


def silu_grad(values):
    sigmoid_value = jax.nn.sigmoid(values)
    return sigmoid_value * (1.0 + values * (1.0 - sigmoid_value))


def octet(volume):
    return volume.reshape(volume.shape[0], volume.shape[1], 2, 2, 2, 4, 4, 4)


def face_of(cube, axis_number, upper):
    number, channels = (cube.shape[0], cube.shape[1])
    plane = lax.index_in_dim(cube, 3 if upper else 0, 5 + axis_number, keepdims=False)
    plane = lax.index_in_dim(plane, 1 if upper else 0, 2 + axis_number, keepdims=False)
    return plane.reshape(number, channels * 64)


def face_index(axis_number, upper):
    index = [slice(None)] * 8
    index[2 + axis_number] = 1 if upper else 0
    index[5 + axis_number] = 3 if upper else 0
    return tuple(index)


def expand_plane(rows, cube, axis_number):
    number, channels = (cube.shape[0], cube.shape[1])
    return jnp.expand_dims(
        rows.reshape(number, channels, 2, 2, 4, 4), (2 + axis_number, 5 + axis_number)
    )


def shift_minus(cube, rows, axis_number):
    parity, place = (2 + axis_number, 5 + axis_number)
    plane = expand_plane(rows, cube, axis_number)
    lower = lax.slice_in_dim(cube, 0, 1, axis=parity)
    upper = lax.slice_in_dim(cube, 1, 2, axis=parity)
    out_low = jnp.concatenate([plane, lax.slice_in_dim(upper, 0, 3, axis=place)], axis=place)
    return jnp.concatenate([out_low, lower], axis=parity)


def shift_plus(cube, rows, axis_number):
    parity, place = (2 + axis_number, 5 + axis_number)
    plane = expand_plane(rows, cube, axis_number)
    lower = lax.slice_in_dim(cube, 0, 1, axis=parity)
    upper = lax.slice_in_dim(cube, 1, 2, axis=parity)
    out_high = jnp.concatenate([lax.slice_in_dim(lower, 1, 4, axis=place), plane], axis=place)
    return jnp.concatenate([upper, out_high], axis=parity)


def minus_back(grad_out, axis_number):
    parity, place = (2 + axis_number, 5 + axis_number)
    grad_low = lax.slice_in_dim(grad_out, 0, 1, axis=parity)
    grad_high = lax.slice_in_dim(grad_out, 1, 2, axis=parity)
    moved = jnp.concatenate(
        [
            lax.slice_in_dim(grad_low, 1, 4, axis=place),
            jnp.zeros_like(lax.slice_in_dim(grad_low, 0, 1, axis=place)),
        ],
        axis=place,
    )
    plane = lax.index_in_dim(
        lax.index_in_dim(grad_low, 0, place, keepdims=False), 0, parity, keepdims=False
    )
    return (jnp.concatenate([grad_high, moved], axis=parity), plane)


def plus_back(grad_out, axis_number):
    parity, place = (2 + axis_number, 5 + axis_number)
    grad_low = lax.slice_in_dim(grad_out, 0, 1, axis=parity)
    grad_high = lax.slice_in_dim(grad_out, 1, 2, axis=parity)
    moved = jnp.concatenate(
        [
            jnp.zeros_like(lax.slice_in_dim(grad_high, 0, 1, axis=place)),
            lax.slice_in_dim(grad_high, 0, 3, axis=place),
        ],
        axis=place,
    )
    plane = lax.index_in_dim(
        lax.index_in_dim(grad_high, 3, place, keepdims=False), 0, parity, keepdims=False
    )
    return (jnp.concatenate([moved, grad_low], axis=parity), plane)


def face_layers(cube):
    return (
        face_of(cube, 0, True),
        face_of(cube, 0, False),
        face_of(cube, 1, True),
        face_of(cube, 1, False),
        face_of(cube, 2, True),
        face_of(cube, 2, False),
    )


def pick_rows(local_rows, remote_rows, index):
    width = local_rows.shape[1]
    pooled = jnp.concatenate(
        [local_rows, remote_rows, jnp.zeros((1, width), local_rows.dtype)], axis=0
    )
    return pooled[index]


def neighbour_stack(cube, faces, remotes, links):
    number, channels = (cube.shape[0], cube.shape[1])
    blank = jnp.zeros_like(faces[4])
    sources = (remotes[0], remotes[1], remotes[2], remotes[3], blank, blank)
    picked = [
        pick_rows(faces[direction], sources[direction], links[:, direction])
        for direction in range(6)
    ]
    fields = [
        cube,
        shift_minus(cube, picked[0], 0),
        shift_plus(cube, picked[1], 0),
        shift_minus(cube, picked[2], 1),
        shift_plus(cube, picked[3], 1),
        shift_minus(cube, picked[4], 2),
        shift_plus(cube, picked[5], 2),
    ]
    return jnp.stack(fields, axis=1).reshape(number, 7 * channels, 512)


def stack_grad(taps_grad, links):
    number, channels = (taps_grad.shape[0], taps_grad.shape[1] // 7)
    parts = taps_grad.reshape(number, 7, channels, 2, 2, 2, 4, 4, 4)
    grad_cube = parts[:, 0]
    face_grads = []
    for direction in range(6):
        axis_number = direction // 2
        if direction % 2 == 0:
            moved, plane = minus_back(parts[:, direction + 1], axis_number)
        else:
            moved, plane = plus_back(parts[:, direction + 1], axis_number)
        grad_cube = grad_cube + moved
        face_grads.append(plane.reshape(number, channels * 64))
    pools = [
        jnp.zeros((2 * number + 1, channels * 64), jnp.float32)
        .at[links[:, direction]]
        .add(face_grads[direction])
        for direction in range(6)
    ]
    for direction in range(6):
        shaped = pools[direction][:number].reshape(number, channels, 2, 2, 4, 4)
        grad_cube = grad_cube.at[face_index(direction // 2, direction % 2 == 0)].add(shaped)
    far_rows = [
        pools[direction][number : 2 * number].astype(jnp.bfloat16) for direction in range(4)
    ]
    return (grad_cube, far_rows)


def add_faces(grad_cube, into_xhigh, into_xlow, into_yhigh, into_ylow):
    number, channels = (grad_cube.shape[0], grad_cube.shape[1])

    def planes(rows):
        return rows.astype(jnp.float32).reshape(number, channels, 2, 2, 4, 4)

    grad_cube = grad_cube.at[face_index(0, True)].add(planes(into_xhigh))
    grad_cube = grad_cube.at[face_index(0, False)].add(planes(into_xlow))
    grad_cube = grad_cube.at[face_index(1, True)].add(planes(into_yhigh))
    grad_cube = grad_cube.at[face_index(1, False)].add(planes(into_ylow))
    return grad_cube


def merge_pool(own_rows):
    beside_y = from_partner(own_rows, "gy", 0)
    received = from_partner(jnp.concatenate([own_rows, beside_y], axis=0), "gx", 0)
    half = own_rows.shape[0]
    return jnp.concatenate([own_rows, received[:half], beside_y, received[half:]], axis=0)


def split_pool(back_rows):
    half = back_rows.shape[0] // 4
    own_part = back_rows[:half].astype(jnp.float32)
    along_x = back_rows[half : 2 * half]
    along_y = back_rows[2 * half : 3 * half]
    diagonal = back_rows[3 * half :]
    returned = from_partner(jnp.concatenate([along_x, diagonal], axis=0), "gx", 0)
    kept = own_part + returned[:half].astype(jnp.float32)
    beside = (along_y.astype(jnp.float32) + returned[half:].astype(jnp.float32)).astype(
        jnp.bfloat16
    )
    final_rows = kept + from_partner(beside, "gy", 0).astype(jnp.float32)
    return final_rows.astype(jnp.bfloat16)


def scatter_rows(volume, links, number):
    width = volume.shape[1] * volume.shape[2] // 8
    rows = volume.reshape(volume.shape[0] * 8, width)
    total = (
        jnp.zeros((4 * number + 1, width), jnp.float32)
        .at[links.reshape(-1)]
        .add(rows.astype(jnp.float32))
    )
    return total[: 4 * number].astype(jnp.bfloat16)


def body(
    features, neighbours, counts, conv_weight, down_weight, head_weight, coarse_map, latent_grad
):
    number, channels = (features.shape[0], features.shape[1])
    wide = down_weight.shape[0]
    coarse_count = coarse_map.shape[0]
    active = jnp.arange(number) < counts[0]
    masked = jnp.where(active[:, None, None], features, jnp.zeros((), jnp.bfloat16))
    cube = octet(masked)
    faces = face_layers(cube)
    rim_x = padded(jnp.stack([faces[1], faces[0]]), (("gx", 0),), 1)
    rim_y = padded(jnp.stack([faces[3], faces[2]]), (("gy", 0),), 1)
    taps = neighbour_stack(cube, faces, (rim_x[0], rim_x[3], rim_y[0], rim_y[3]), neighbours)
    hidden = jnp.einsum("ok,bkv->bov", conv_weight, taps, preferred_element_type=jnp.float32)
    act = jax.nn.silu(hidden).astype(jnp.bfloat16)
    patches = act.reshape(number, channels * 8, 64)
    octants = jnp.einsum(
        "ok,bkv->bvo", down_weight, patches, preferred_element_type=jnp.float32
    ).astype(jnp.bfloat16)
    empty_row = jnp.zeros((1, 64 * wide), jnp.bfloat16)
    merged = merge_pool(octants.reshape(number, 64 * wide))
    coarse = jnp.concatenate([merged, empty_row], axis=0)[coarse_map].reshape(
        coarse_count, 512, wide
    )
    coarse_act = jax.nn.silu(coarse.astype(jnp.float32)).astype(jnp.bfloat16)
    latent = jnp.einsum(
        "oi,cvi->cvo", head_weight, coarse_act, preferred_element_type=jnp.float32
    ).astype(jnp.bfloat16)
    act_grad = jnp.einsum(
        "oi,cvo->cvi", head_weight, latent_grad, preferred_element_type=jnp.float32
    )
    coarse_grad = (act_grad * silu_grad(coarse.astype(jnp.float32))).astype(jnp.bfloat16)
    head_part = jnp.einsum(
        "cvo,cvi->oi", latent_grad, coarse_act, preferred_element_type=jnp.float32
    )
    octant_grad = split_pool(scatter_rows(coarse_grad, coarse_map, number)).reshape(
        number, 64, wide
    )
    down_part = jnp.einsum("bvo,bkv->ok", octant_grad, patches, preferred_element_type=jnp.float32)
    patch_grad = jnp.einsum(
        "ok,bvo->bkv", down_weight, octant_grad, preferred_element_type=jnp.float32
    )
    hidden_grad = (patch_grad.reshape(number, channels, 512) * silu_grad(hidden)).astype(
        jnp.bfloat16
    )
    conv_part = jnp.einsum("bov,bkv->ok", hidden_grad, taps, preferred_element_type=jnp.float32)
    taps_grad = jnp.einsum(
        "ok,bov->bkv", conv_weight, hidden_grad, preferred_element_type=jnp.float32
    )
    near_grad, far_rows = stack_grad(taps_grad, neighbours)
    return_x = padded(jnp.stack([far_rows[0], far_rows[1]]), (("gx", 0),), 1)
    return_y = padded(jnp.stack([far_rows[2], far_rows[3]]), (("gy", 0),), 1)
    total_grad = add_faces(near_grad, return_x[3], return_x[0], return_y[3], return_y[0]).reshape(
        number, channels, 512
    )
    features_grad = jnp.where(active[:, None, None], total_grad, 0.0).astype(jnp.bfloat16)
    summed = lax.psum((conv_part, down_part, head_part), ("gx", "gy"))
    scale = float(number * lax.axis_size("gx") * lax.axis_size("gy")) ** (-0.5)
    return (latent, features_grad, summed[0] * scale, summed[1] * scale, summed[2] * scale)


def solution(mesh):
    placed = (
        P(("gx", "gy"), None, None),
        P(("gx", "gy"), None),
        P(("gx", "gy")),
        P(),
        P(),
        P(),
        P(("gx", "gy"), None),
        P(("gx", "gy"), None, None),
    )
    return jax.shard_map(
        body,
        mesh=mesh,
        in_specs=placed,
        out_specs=(P(("gx", "gy"), None, None), P(("gx", "gy"), None, None), P(), P(), P()),
        check_vma=False,
    )
```

profile of v0, /device:TPU:2, one launch (start us, length us, event | category | flops | bytes accessed | tf_op | source)
XLA Modules:
  0.0 611.6 jit_solution(5561831385059505792)
XLA Ops:
  12.5 4.4 collective-permute-start
  21.6 3.1 copy.127
  29.4 3.1 copy.134
  34.7 3.8 collective-permute-start.3
  90.8 11.2 %copy.151 = bf16[8,7,64,2,2,2,4,4,4]{2,1,8,7,6,5,4,3,0:T(8,128)(2,1)} copy(bf16[8,7,64,2,2,2,4,4,4]{2,0,8,7,6,5,4,3,1:T(8,128)(2,1)} %fusion.16) | data formatting | bytes 7340032 | tf_op jit(solution)/shard_map/stack | solution.py:148
  102.0 11.6 %reshape.747 = bf16[8,448,512]{1,2,0:T(8,128)(2,1)} reshape(bf16[8,7,64,2,2,2,4,4,4]{2,1,8,7,6,5,4,3,0:T(8,128)(2,1)} %copy.151) | data formatting | bytes 7340032 | tf_op jit(solution)/shard_map/reshape | solution.py:148
  113.6 4.6 multiply_convert_fusion.1
  120.8 2.7 collective-permute-start.5
  123.7 6.5 %collective-permute-done.5 = bf16[16,8192]{1,0:T(8,128)(2,1)S(1)} collective-permute-done((bf16[16,8192]{1,0:T(8,128)(2,1)S(1)}, bf16[16,8192]{1,0:T(8,128)(2,1)S(1)}, u32[]{:S(2)}, u32[]{:S(2)}) %collective-permute-start.5) | collective-permute-done | bytes 262176 | tf_op jit(solution)/shard_map/ppermute | solution.py:14
  136.6 4.1 collective-permute-done.6
  148.8 3.7 convolution_bitcast_fusion.4
  152.5 4.1 convolution_bitcast_fusion
  156.6 8.8 %copy.155 = f32[8,448,512]{1,2,0:T(8,128)} copy(f32[8,448,512]{2,1,0:T(8,128)} %convolution_bitcast_fusion) | data formatting | bytes 14680064 | tf_op jit(solution)/shard_map/ok,bov->bkv/transpose | solution.py:271
  165.4 13.2 %reshape.754 = f32[8,7,64,2,2,2,4,4,4]{2,1,8,7,6,5,4,3,0:T(8,128)} reshape(f32[8,448,512]{1,2,0:T(8,128)} %copy.155) | data formatting | bytes 14680064 | tf_op jit(solution)/shard_map/reshape | solution.py:153
  178.6 53.0 %fusion.67 = (f32[8,1,64,2,2,2,4,4,4]{2,1,8,7,6,5,4,3,0:T(1,128)S(1)}, f32[8,1,64,2,2,2,4,4,4]{2,1,8,7,6,5,4,3,0:T(1,128)S(1)}, f32[8,1,64,2,2,2,4,4,4]{2,1,8,7,...) fusion(f32[8,7,64,2,2,2,4,4,4]{2,1,8,7,6,5,4,3,0:T(8,128)} %res, ...), kind=kLoop, calls=%fused_computation.173 | loop fusion | bytes 14680064 | tf_op jit(solution)/shard_map/slice | solution.py:159
  249.3 3.1 copy.166
  254.7 3.2 copy.170
  260.1 3.2 copy.162
  267.0 3.1 copy.174
  273.9 3.1 copy.178
  280.2 3.1 copy.182
  286.5 4.0 collective-permute-start.9
  293.7 2.6 collective-permute-start.11
  313.6 6.5 %fusion = f32[8,64,2,2,2,4,4,4]{1,7,6,5,4,3,2,0:T(4,128)S(1)} fusion(f32[8,64,2,2,1,4,4,3]{1,7,6,5,4,3,2,0:T(4,128)} %slice.902, f32[8,64,2,2,1,4,4,3]{1,7,6,5,4,3,2,0:T(4,128)} %slice.900, f32[8,64,2,1,2,4,3,4]{1,7,6,5,4,3,2,0:T(4,128)} %slice.896, f32[8,64,2,1,2,4,3,4]{1,7,6,5,4,3,2,0:T(4,128)} %slice.894, f32[8,64,1,2,2,3,4,4]{1,7,6,5,4,3,2,0:T(4,128)} %slice.890, ...), kind=kLoop, calls=%fused_computation.16 | loop fusion | flops 6291456 | bytes 7602176 | tf_op jit(solution)/shard_map/add | solution.py:162
  322.3 6.4 %scatter-add.109 = f32[8,64,2,2,2,4,4,4]{1,7,6,5,4,3,2,0:T(4,128)S(1)} dynamic-update-slice(f32[8,64,2,2,2,4,4,4]{1,7,6,5,4,3,2,0:T(4,128)S(1)} %fusion.23, f32[8,64,2,2,1,4,4,1]{1,7,6,5,4,3,2,0:T(1,128)} %slice_add_fusion.5, s32[]{:T(128)} %constant.277.clone.1, s32[]{:T(128)} %constant.277.clone.1, s32[]{:T(128)} %constant.277.clone.1, s32[]{:T(128)} %constant.277.clone.1, s32[]{:T(128)} %constant.282.clone.1, ...) | dynamic-update-slice | bytes 262148 | tf_op jit(solution)/shard_map/scatter-add | solution.py:172
  331.8 6.4 %scatter-add.111 = f32[8,64,2,2,2,4,4,4]{1,7,6,5,4,3,2,0:T(4,128)S(1)} dynamic-update-slice(f32[8,64,2,2,2,4,4,4]{1,7,6,5,4,3,2,0:T(4,128)S(1)} %scatter-add.109, f32[8,64,2,2,1,4,4,1]{1,7,6,5,4,3,2,0:T(1,128)} %slice_add_fusion.4, s32[]{:T(128)} %constant.277.clone.1, s32[]{:T(128)} %constant.277.clone.1, s32[]{:T(128)} %constant.277.clone.1, s32[]{:T(128)} %constant.277.clone.1, ...) | dynamic-update-slice | bytes 262148 | tf_op jit(solution)/shard_map/scatter-add | solution.py:172
  338.2 2.5 copy.192
  343.2 2.5 copy.186
  348.1 2.5 copy.190
  350.6 2.6 copy.191
  353.3 2.5 copy.188
  361.8 237.7 %all-reduce.9.cloned.1.call-done = (f32[64,448]{1,0:T(8,128)}, f32[128,512]{1,0:T(8,128)}, f32[128,128]{0,1:T(8,128)}) async-done(((f32[64,448]{1,0:T(8,128)}, f32[128,512]{1,0:T(8,128)}, f32[128,128]{0,1:T(8,128)}), (f32[64,448]{1,0:T(8,128)}, f32[128,512]{1,0:T(8,128)}, f32[128,128]{0,1:T(8,128)})) %all-reduce.9.cloned.1.call-update) | async-done | bytes 442384 | tf_op jit(solution)/shard_map/psum | solution.py:281
  (287 shorter events, 162.1 us)
Async XLA Ops:
  7.2 111.6 %copy-start = (bf16[128,512]{1,0:T(8,128)(2,1)S(1)}, bf16[128,512]{1,0:T(8,128)(2,1)}, u32[]{:S(2)}) copy-start(bf16[128,512]{1,0:T(8,128)(2,1)} %param.32) | copy-start | bytes 393220
  7.2 592.3 %all-reduce.9.cloned.1.call-start = ((), (), s32[]{:S(2)}) async-start(), calls=%async_computation | async-start | bytes 917504 | tf_op jit(solution)/shard_map/psum | solution.py:281
  12.5 52.6 %collective-permute-start = (bf16[1,8,4096]{2,1,0:T(8,128)(2,1)}, bf16[1,8,4096]{2,1,0:T(8,128)(2,1)}, u32[]{:S(2)}, u32[]{:S(2)}) collective-permute-start(bf16[1,8,4096]{2,1,0:T(8,128)(2,1)} %copy.115), channel_id=1, source_target_pairs={{0,8},{8,16},{16,24},{24,32},{32,40},{40,48},{48,56},{56,64},{64,7... | collective-permute-start | bytes 196616 | tf_op jit(solution)/shard_map/ppermute | solution.py:22
  19.6 45.6 %collective-permute-start.1 = (bf16[1,8,4096]{2,1,0:T(8,128)(2,1)}, bf16[1,8,4096]{2,1,0:T(8,128)(2,1)}, u32[]{:S(2)}, u32[]{:S(2)}) collective-permute-start(bf16[1,8,4096]{2,1,0:T(8,128)(2,1)} %copy.122), channel_id=1, source_target_pairs={{8,0},{16,8},{24,16},{32,24},{40,32},{48,40},{56,48},{64,56},{72,6... | collective-permute-start | bytes 196616 | tf_op jit(solution)/shard_map/ppermute | solution.py:25
  26.8 38.3 %collective-permute-start.2 = (bf16[1,8,4096]{2,1,0:T(8,128)(2,1)}, bf16[1,8,4096]{2,1,0:T(8,128)(2,1)}, u32[]{:S(2)}, u32[]{:S(2)}) collective-permute-start(bf16[1,8,4096]{2,1,0:T(8,128)(2,1)} %copy.129), channel_id=1, source_target_pairs={{0,1},{1,2},{2,3},{3,4},{4,5},{5,6},{6,7},{8,9},{9,10},{10,11},{11... | collective-permute-start | bytes 196616 | tf_op jit(solution)/shard_map/ppermute | solution.py:22
  34.7 30.5 %collective-permute-start.3 = (bf16[1,8,4096]{2,1,0:T(8,128)(2,1)}, bf16[1,8,4096]{2,1,0:T(8,128)(2,1)}, u32[]{:S(2)}, u32[]{:S(2)}) collective-permute-start(bf16[1,8,4096]{2,1,0:T(8,128)(2,1)} %copy.136), channel_id=1, source_target_pairs={{1,0},{2,1},{3,2},{4,3},{5,4},{6,5},{7,6},{9,8},{10,9},{11,10},{12... | collective-permute-start | bytes 196616 | tf_op jit(solution)/shard_map/ppermute | solution.py:25
  43.3 3.9 copy-start.26
  58.3 3.8 copy-start.24
  62.1 3.0 copy-start.32
  62.1 3.1 copy-start.38
  62.2 3.1 copy-start.39
  77.0 6.0 copy-start.8
  77.0 6.0 copy-start.14
  79.4 4.9 copy-start.7
  79.4 4.9 copy-start.13
  102.0 11.6 %copy-start.28 = (bf16[64,448]{1,0:T(8,128)(2,1)S(1)}, bf16[64,448]{1,0:T(8,128)(2,1)}, u32[]{:S(2)}) copy-start(bf16[64,448]{1,0:T(8,128)(2,1)} %param.31) | copy-start | bytes 172036
  118.8 12.2 %copy-start.27 = (bf16[1,512,128]{2,1,0:T(8,128)(2,1)S(1)}, bf16[1,512,128]{2,1,0:T(8,128)(2,1)}, u32[]{:S(2)}) copy-start(bf16[1,512,128]{2,1,0:T(8,128)(2,1)} %param.35) | copy-start | bytes 393220
  118.8 12.2 %copy-start.40 = (bf16[128,128]{1,0:T(8,128)(2,1)S(1)}, bf16[128,128]{1,0:T(8,128)(2,1)}, u32[]{:S(2)}) copy-start(bf16[128,128]{1,0:T(8,128)(2,1)} %param.33) | copy-start | bytes 98308
  119.4 1.4 collective-permute-start.4
  120.8 9.4 %collective-permute-start.5 = (bf16[16,8192]{1,0:T(8,128)(2,1)S(1)}, bf16[16,8192]{1,0:T(8,128)(2,1)S(1)}, u32[]{:S(2)}, u32[]{:S(2)}) collective-permute-start(bf16[16,8192]{1,0:T(8,128)(2,1)S(1)} %pad_maximum_fusion), channel_id=1, source_target_pairs={{0,8},{8,0},{16,24},{24,16},{32,40},{40,32},{48,56},{56,48},{64,72... | collective-permute-start | bytes 786440 | tf_op jit(solution)/shard_map/ppermute | solution.py:14
  132.7 8.3 %copy-start.41 = (bf16[128,128]{1,0:T(8,128)(2,1)S(1)}, bf16[128,128]{1,0:T(8,128)(2,1)}, u32[]{:S(2)}) copy-start(bf16[128,128]{1,0:T(8,128)(2,1)} %param.33) | copy-start | bytes 98308
  132.7 8.0 %collective-permute-start.6 = (bf16[16,8192]{1,0:T(8,128)(2,1)S(1)}, bf16[16,8192]{1,0:T(8,128)(2,1)S(1)}, u32[]{:S(2)}, u32[]{:S(2)}) collective-permute-start(bf16[16,8192]{1,0:T(8,128)(2,1)S(1)} %pad_maximum_fusion.1), channel_id=1, source_target_pairs={{0,8},{8,0},{16,24},{24,16},{32,40},{40,32},{48,56},{56,48},{64,72... | collective-permute-start | bytes 786440 | tf_op jit(solution)/shard_map/ppermute | solution.py:14
  140.8 1.4 collective-permute-start.7
  148.8 3.7 copy-start.29
  286.5 66.8 %collective-permute-start.9 = (bf16[1,8,4096]{2,1,0:T(8,128)(2,1)}, bf16[1,8,4096]{2,1,0:T(8,128)(2,1)}, u32[]{:S(2)}, u32[]{:S(2)}) collective-permute-start(bf16[1,8,4096]{2,1,0:T(8,128)(2,1)} %fusion.53), channel_id=1, source_target_pairs={{0,8},{8,16},{16,24},{24,32},{32,40},{40,48},{48,56},{56,64},{64,7... | collective-permute-start | bytes 196616 | tf_op jit(solution)/shard_map/ppermute | solution.py:22
  290.5 57.6 %collective-permute-start.10 = (bf16[1,8,4096]{2,1,0:T(8,128)(2,1)}, bf16[1,8,4096]{2,1,0:T(8,128)(2,1)}, u32[]{:S(2)}, u32[]{:S(2)}) collective-permute-start(bf16[1,8,4096]{2,1,0:T(8,128)(2,1)} %fusion.54), channel_id=1, source_target_pairs={{1,0},{2,1},{3,2},{4,3},{5,4},{6,5},{7,6},{9,8},{10,9},{11,10},{12... | collective-permute-start | bytes 196616 | tf_op jit(solution)/shard_map/ppermute | solution.py:25
  292.4 50.8 %collective-permute-start.8 = (bf16[1,8,4096]{2,1,0:T(8,128)(2,1)}, bf16[1,8,4096]{2,1,0:T(8,128)(2,1)}, u32[]{:S(2)}, u32[]{:S(2)}) collective-permute-start(bf16[1,8,4096]{2,1,0:T(8,128)(2,1)} %fusion.52), channel_id=1, source_target_pairs={{8,0},{16,8},{24,16},{32,24},{40,32},{48,40},{56,48},{64,56},{72,6... | collective-permute-start | bytes 196616 | tf_op jit(solution)/shard_map/ppermute | solution.py:25
  293.7 44.5 %collective-permute-start.11 = (bf16[1,8,4096]{2,1,0:T(8,128)(2,1)}, bf16[1,8,4096]{2,1,0:T(8,128)(2,1)}, u32[]{:S(2)}, u32[]{:S(2)}) collective-permute-start(bf16[1,8,4096]{2,1,0:T(8,128)(2,1)} %fusion.55), channel_id=1, source_target_pairs={{0,1},{1,2},{2,3},{3,4},{4,5},{5,6},{6,7},{8,9},{9,10},{10,11},{11... | collective-permute-start | bytes 196616 | tf_op jit(solution)/shard_map/ppermute | solution.py:22
  313.6 6.5 %copy-start.17 = (f32[8,64,1,2,2,1,4,4]{1,7,6,5,4,3,2,0:T(4,128)S(1)}, f32[8,64,1,2,2,1,4,4]{1,7,6,5,4,3,2,0:T(4,128)}, u32[]{:S(2)}) copy-start(f32[8,64,1,2,2,1,4,4]{1,7,6,5,4,3,2,0:T(4,128)} %copy.165) | copy-start | bytes 393220
  313.6 6.7 %copy-start.19 = (f32[8,64,1,2,2,1,4,4]{1,7,6,5,4,3,2,0:T(4,128)S(1)}, f32[8,64,1,2,2,1,4,4]{1,7,6,5,4,3,2,0:T(4,128)}, u32[]{:S(2)}) copy-start(f32[8,64,1,2,2,1,4,4]{1,7,6,5,4,3,2,0:T(4,128)} %copy.169) | copy-start | bytes 393220
  313.6 6.8 %copy-start.16 = (f32[8,64,2,1,2,4,1,4]{1,7,6,5,4,3,2,0:T(4,128)S(1)}, f32[8,64,2,1,2,4,1,4]{1,7,6,5,4,3,2,0:T(4,128)}, u32[]{:S(2)}) copy-start(f32[8,64,2,1,2,4,1,4]{1,7,6,5,4,3,2,0:T(4,128)} %copy.173) | copy-start | bytes 393220
  358.7 245.6 %copy-start.1 = (bf16[128,512]{1,0:T(8,128)(2,1)S(1)}, bf16[128,512]{1,0:T(8,128)(2,1)}, u32[]{:S(2)}) copy-start(bf16[128,512]{1,0:T(8,128)(2,1)} %param.32) | copy-start | bytes 393220
  (25 other events, 49.3 us)
Sparse Core Ops, SparseCore 0:
  338.3 261.1 all-reduce.8
where the time goes:
time: 619 us; the launch traced here: 612 us
  local copies, waits for them, and re-layouts  264 us (43%)
  waiting for transfers between devices  250 us (40%)
  other arithmetic  37.3 us (6%)
  starting transfers between devices  26.2 us (4%)
  matrix products  18.1 us (3%)
  between operations  16.2 us (3%)
    psum x1, waiting for transfers between devices, body(): summed = lax.psum((conv_part, down_part, head_part), ('gx', 'gy'))  238 us
    slice x1, local copies, waits for them, and re-layouts, stack_grad(): moved, plane = minus_back(parts[:, direction + 1], axis_number)  53 us
    convert_element_type x8, local copies, waits for them, and re-layouts, planes(): return rows.astype(jnp.float32).reshape(number, channels, 2, 2, 4, 4)  20 us
    slice x12, local copies, waits for them, and re-layouts, face_of(): lax.index_in_dim(plane, 1 if upper else 0, 2 + axis_number, keepdims=False)  16.3 us
    reshape x1, local copies, waits for them, and re-layouts, stack_grad(): parts = taps_grad.reshape(number, 7, channels, 2, 2, 2, 4, 4, 4)  13.2 us
    ppermute x4, starting transfers between devices, padded(): lax.ppermute(lax.slice_in_dim(block, block.shape[dim] - width, None, axis...  12.9 us
    scatter-add x2, local copies, waits for them, and re-layouts, stack_grad(): grad_cube.at[face_index(direction // 2, direction % 2 == 0)].add(shaped)  12.7 us
    ppermute x4, waiting for transfers between devices, from_partner(): return lax.ppermute(block, axis, route)  12.4 us
  transfers between devices with their start and end apart: 13, of which 5 were waited for; matrix products, arithmetic and copies ran while one was open for 18% of the time, Pallas kernels for 0%

commit v1 on v0

--- a/solution.py
+++ b/solution.py
@@ -278,7 +278,7 @@
         number, channels, 512
     )
     features_grad = jnp.where(active[:, None, None], total_grad, 0.0).astype(jnp.bfloat16)
-    summed = lax.psum((conv_part, down_part, head_part), ("gx", "gy"))
+    summed = lax.psum(lax.psum((conv_part, down_part, head_part), "gx"), "gy")
     scale = float(number * lax.axis_size("gx") * lax.axis_size("gy")) ** (-0.5)
     return (latent, features_grad, summed[0] * scale, summed[1] * scale, summed[2] * scale)
 

time: 619 us -> 579 us (0.935)
  waiting for transfers between devices: 250 us -> 207 us
    psum x1 -> x2, waiting for transfers between devices: 238 us -> 195 us  [body(): summed = lax.psum(lax.psum((conv_part, down_part, head_part), 'gx'), 'gy')]
  transfers between devices with their start and end apart: 13 -> 14, of which waited for: 5 -> 6; matrix products, arithmetic and copies ran while one was open for 18% -> 19% of each run, Pallas kernels for 0% -> 0%
where the time goes in v1:
time: 579 us; the launch traced here: 569 us
  local copies, waits for them, and re-layouts  264 us (46%)
  waiting for transfers between devices  207 us (36%)
  other arithmetic  37.6 us (6%)
  starting transfers between devices  26.3 us (5%)
  matrix products  18.1 us (3%)
  between operations  16.2 us (3%)
    psum x2, waiting for transfers between devices, body(): summed = lax.psum(lax.psum((conv_part, down_part, head_part), 'gx'), 'gy')  195 us
    slice x1, local copies, waits for them, and re-layouts, stack_grad(): moved, plane = minus_back(parts[:, direction + 1], axis_number)  53.6 us
    convert_element_type x8, local copies, waits for them, and re-layouts, planes(): return rows.astype(jnp.float32).reshape(number, channels, 2, 2, 4, 4)  19.7 us
    slice x12, local copies, waits for them, and re-layouts, face_of(): lax.index_in_dim(plane, 1 if upper else 0, 2 + axis_number, keepdims=False)  16.3 us
    reshape x1, local copies, waits for them, and re-layouts, stack_grad(): parts = taps_grad.reshape(number, 7, channels, 2, 2, 2, 4, 4, 4)  13.2 us
    ppermute x4, starting transfers between devices, padded(): lax.ppermute(lax.slice_in_dim(block, block.shape[dim] - width, None, axis...  12.7 us
    scatter-add x2, local copies, waits for them, and re-layouts, stack_grad(): grad_cube.at[face_index(direction // 2, direction % 2 == 0)].add(shaped)  12.7 us
    ppermute x4, waiting for transfers between devices, from_partner(): return lax.ppermute(block, axis, route)  12.4 us
  transfers between devices with their start and end apart: 14, of which 6 were waited for; matrix products, arithmetic and copies ran while one was open for 19% of the time, Pallas kernels for 0%

profile of v1, /device:TPU:2, one launch (start us, length us, event | category | flops | bytes accessed | tf_op | source)
XLA Modules:
  0.0 569.5 jit_solution(3019619345830593339)
XLA Ops:
  12.6 4.5 collective-permute-start
  21.6 3.1 copy.127
  29.5 3.1 copy.134
  34.8 3.8 collective-permute-start.3
  90.9 11.2 %copy.151 = bf16[8,7,64,2,2,2,4,4,4]{2,1,8,7,6,5,4,3,0:T(8,128)(2,1)} copy(bf16[8,7,64,2,2,2,4,4,4]{2,0,8,7,6,5,4,3,1:T(8,128)(2,1)} %fusion.16) | data formatting | bytes 7340032 | tf_op jit(solution)/shard_map/stack | solution.py:148
  102.2 11.6 %reshape.747 = bf16[8,448,512]{1,2,0:T(8,128)(2,1)} reshape(bf16[8,7,64,2,2,2,4,4,4]{2,1,8,7,6,5,4,3,0:T(8,128)(2,1)} %copy.151) | data formatting | bytes 7340032 | tf_op jit(solution)/shard_map/reshape | solution.py:148
  113.8 4.6 multiply_convert_fusion.1
  121.0 2.7 collective-permute-start.5
  123.8 6.5 %collective-permute-done.5 = bf16[16,8192]{1,0:T(8,128)(2,1)S(1)} collective-permute-done((bf16[16,8192]{1,0:T(8,128)(2,1)S(1)}, bf16[16,8192]{1,0:T(8,128)(2,1)S(1)}, u32[]{:S(2)}, u32[]{:S(2)}) %collective-permute-start.5) | collective-permute-done | bytes 262176 | tf_op jit(solution)/shard_map/ppermute | solution.py:14
  136.8 4.1 collective-permute-done.6
  148.9 3.7 convolution_bitcast_fusion.4
  152.7 4.1 convolution_bitcast_fusion
  156.7 8.8 %copy.155 = f32[8,448,512]{1,2,0:T(8,128)} copy(f32[8,448,512]{2,1,0:T(8,128)} %convolution_bitcast_fusion) | data formatting | bytes 14680064 | tf_op jit(solution)/shard_map/ok,bov->bkv/transpose | solution.py:271
  165.6 13.2 %reshape.754 = f32[8,7,64,2,2,2,4,4,4]{2,1,8,7,6,5,4,3,0:T(8,128)} reshape(f32[8,448,512]{1,2,0:T(8,128)} %copy.155) | data formatting | bytes 14680064 | tf_op jit(solution)/shard_map/reshape | solution.py:153
  178.7 53.6 %fusion.67 = (f32[8,1,64,2,2,2,4,4,4]{2,1,8,7,6,5,4,3,0:T(1,128)S(1)}, f32[8,1,64,2,2,2,4,4,4]{2,1,8,7,6,5,4,3,0:T(1,128)S(1)}, f32[8,1,64,2,2,2,4,4,4]{2,1,8,7,...) fusion(f32[8,7,64,2,2,2,4,4,4]{2,1,8,7,6,5,4,3,0:T(8,128)} %res, ...), kind=kLoop, calls=%fused_computation.173 | loop fusion | bytes 14680064 | tf_op jit(solution)/shard_map/slice | solution.py:159
  250.2 3.1 copy.166
  255.5 3.2 copy.170
  261.1 3.2 copy.162
  268.0 3.1 copy.174
  275.0 3.1 copy.178
  281.2 3.1 copy.182
  287.5 4.0 collective-permute-start.9
  294.7 2.4 collective-permute-start.11
  314.3 6.5 %fusion = f32[8,64,2,2,2,4,4,4]{1,7,6,5,4,3,2,0:T(4,128)S(1)} fusion(f32[8,64,2,2,1,4,4,3]{1,7,6,5,4,3,2,0:T(4,128)} %slice.902, f32[8,64,2,2,1,4,4,3]{1,7,6,5,4,3,2,0:T(4,128)} %slice.900, f32[8,64,2,1,2,4,3,4]{1,7,6,5,4,3,2,0:T(4,128)} %slice.896, f32[8,64,2,1,2,4,3,4]{1,7,6,5,4,3,2,0:T(4,128)} %slice.894, f32[8,64,1,2,2,3,4,4]{1,7,6,5,4,3,2,0:T(4,128)} %slice.890, ...), kind=kLoop, calls=%fused_computation.16 | loop fusion | flops 6291456 | bytes 7602176 | tf_op jit(solution)/shard_map/add | solution.py:162
  323.1 6.4 %scatter-add.109 = f32[8,64,2,2,2,4,4,4]{1,7,6,5,4,3,2,0:T(4,128)S(1)} dynamic-update-slice(f32[8,64,2,2,2,4,4,4]{1,7,6,5,4,3,2,0:T(4,128)S(1)} %fusion.23, f32[8,64,2,2,1,4,4,1]{1,7,6,5,4,3,2,0:T(1,128)} %slice_add_fusion.5, s32[]{:T(128)} %constant.277.clone.1, s32[]{:T(128)} %constant.277.clone.1, s32[]{:T(128)} %constant.277.clone.1, s32[]{:T(128)} %constant.277.clone.1, s32[]{:T(128)} %constant.282.clone.1, ...) | dynamic-update-slice | bytes 262148 | tf_op jit(solution)/shard_map/scatter-add | solution.py:172
  332.6 6.4 %scatter-add.111 = f32[8,64,2,2,2,4,4,4]{1,7,6,5,4,3,2,0:T(4,128)S(1)} dynamic-update-slice(f32[8,64,2,2,2,4,4,4]{1,7,6,5,4,3,2,0:T(4,128)S(1)} %scatter-add.109, f32[8,64,2,2,1,4,4,1]{1,7,6,5,4,3,2,0:T(1,128)} %slice_add_fusion.4, s32[]{:T(128)} %constant.277.clone.1, s32[]{:T(128)} %constant.277.clone.1, s32[]{:T(128)} %constant.277.clone.1, s32[]{:T(128)} %constant.277.clone.1, ...) | dynamic-update-slice | bytes 262148 | tf_op jit(solution)/shard_map/scatter-add | solution.py:172
  339.3 2.5 copy.192
  344.2 2.5 copy.186
  349.2 2.5 copy.190
  354.2 2.5 copy.188
  360.8 133.0 %all-reduce.11.cloned.1.call-done = (f32[64,448]{1,0:T(8,128)}, f32[128,512]{1,0:T(8,128)}, f32[128,128]{0,1:T(8,128)}) async-done(((f32[64,448]{1,0:T(8,128)}, f32[128,512]{1,0:T(8,128)}, f32[128,128]{0,1:T(8,128)}), (f32[64,448]{1,0:T(8,128)}, f32[128,512]{1,0:T(8,128)}, f32[128,128]{0,1:T(8,128)})) %all-reduce.11.cloned.1.call-update) | async-done | bytes 442384 | tf_op jit(solution)/shard_map/psum | solution.py:281
  495.7 61.7 %all-reduce.13.cloned.1.call-done = (f32[64,448]{1,0:T(8,128)}, f32[128,512]{1,0:T(8,128)}, f32[128,128]{0,1:T(8,128)}) async-done(((f32[64,448]{1,0:T(8,128)}, f32[128,512]{1,0:T(8,128)}, f32[128,128]{0,1:T(8,128)}), (f32[64,448]{1,0:T(8,128)}, f32[128,512]{1,0:T(8,128)}, f32[128,128]{0,1:T(8,128)})) %all-reduce.13.cloned.1.call-update) | async-done | bytes 442384 | tf_op jit(solution)/shard_map/psum | solution.py:281
  (290 shorter events, 165.2 us)
Async XLA Ops:
  7.2 111.7 %copy-start = (bf16[128,512]{1,0:T(8,128)(2,1)S(1)}, bf16[128,512]{1,0:T(8,128)(2,1)}, u32[]{:S(2)}) copy-start(bf16[128,512]{1,0:T(8,128)(2,1)} %param.32) | copy-start | bytes 393220
  7.2 486.6 %all-reduce.11.cloned.1.call-start = ((), (), s32[]{:S(2)}) async-start(), calls=%async_computation | async-start | bytes 917504 | tf_op jit(solution)/shard_map/psum | solution.py:281
  12.6 52.8 %collective-permute-start = (bf16[1,8,4096]{2,1,0:T(8,128)(2,1)}, bf16[1,8,4096]{2,1,0:T(8,128)(2,1)}, u32[]{:S(2)}, u32[]{:S(2)}) collective-permute-start(bf16[1,8,4096]{2,1,0:T(8,128)(2,1)} %copy.115), channel_id=1, source_target_pairs={{0,8},{8,16},{16,24},{24,32},{32,40},{40,48},{48,56},{56,64},{64,7... | collective-permute-start | bytes 196616 | tf_op jit(solution)/shard_map/ppermute | solution.py:22
  19.6 45.8 %collective-permute-start.1 = (bf16[1,8,4096]{2,1,0:T(8,128)(2,1)}, bf16[1,8,4096]{2,1,0:T(8,128)(2,1)}, u32[]{:S(2)}, u32[]{:S(2)}) collective-permute-start(bf16[1,8,4096]{2,1,0:T(8,128)(2,1)} %copy.122), channel_id=1, source_target_pairs={{8,0},{16,8},{24,16},{32,24},{40,32},{48,40},{56,48},{64,56},{72,6... | collective-permute-start | bytes 196616 | tf_op jit(solution)/shard_map/ppermute | solution.py:25
  26.9 38.5 %collective-permute-start.2 = (bf16[1,8,4096]{2,1,0:T(8,128)(2,1)}, bf16[1,8,4096]{2,1,0:T(8,128)(2,1)}, u32[]{:S(2)}, u32[]{:S(2)}) collective-permute-start(bf16[1,8,4096]{2,1,0:T(8,128)(2,1)} %copy.129), channel_id=1, source_target_pairs={{0,1},{1,2},{2,3},{3,4},{4,5},{5,6},{6,7},{8,9},{9,10},{10,11},{11... | collective-permute-start | bytes 196616 | tf_op jit(solution)/shard_map/ppermute | solution.py:22
  34.8 30.6 %collective-permute-start.3 = (bf16[1,8,4096]{2,1,0:T(8,128)(2,1)}, bf16[1,8,4096]{2,1,0:T(8,128)(2,1)}, u32[]{:S(2)}, u32[]{:S(2)}) collective-permute-start(bf16[1,8,4096]{2,1,0:T(8,128)(2,1)} %copy.136), channel_id=1, source_target_pairs={{1,0},{2,1},{3,2},{4,3},{5,4},{6,5},{7,6},{9,8},{10,9},{11,10},{12... | collective-permute-start | bytes 196616 | tf_op jit(solution)/shard_map/ppermute | solution.py:25
  43.4 4.0 copy-start.26
  58.5 3.8 copy-start.24
  62.4 3.1 copy-start.38
  77.2 5.9 %copy-start.8 = (bf16[8,64,1,2,2,4,4,4]{1,0,7,6,5,4,3,2:T(8,128)(2,1)S(1)}, bf16[8,64,1,2,2,4,4,4]{1,0,7,6,5,4,3,2:T(8,128)(2,1)}, u32[]{:S(2)}) copy-start(bf16[8,64,1,2,2,4,4,4]{1,0,7,6,5,4,3,2:T(8,128)(2,1)} %get-tuple-element.166) | copy-start | bytes 786436
  77.2 5.9 %copy-start.14 = (bf16[8,64,1,2,2,3,4,4]{1,0,7,6,5,4,3,2:T(8,128)(2,1)S(1)}, bf16[8,64,1,2,2,3,4,4]{1,0,7,6,5,4,3,2:T(8,128)(2,1)}, u32[]{:S(2)}) copy-start(bf16[8,64,1,2,2,3,4,4]{1,0,7,6,5,4,3,2:T(8,128)(2,1)} %get-tuple-element.168) | copy-start | bytes 589828
  79.6 4.9 copy-start.7
  79.6 4.9 copy-start.13
  102.2 11.6 %copy-start.28 = (bf16[64,448]{1,0:T(8,128)(2,1)S(1)}, bf16[64,448]{1,0:T(8,128)(2,1)}, u32[]{:S(2)}) copy-start(bf16[64,448]{1,0:T(8,128)(2,1)} %param.31) | copy-start | bytes 172036
  118.9 12.2 %copy-start.27 = (bf16[1,512,128]{2,1,0:T(8,128)(2,1)S(1)}, bf16[1,512,128]{2,1,0:T(8,128)(2,1)}, u32[]{:S(2)}) copy-start(bf16[1,512,128]{2,1,0:T(8,128)(2,1)} %param.35) | copy-start | bytes 393220
  118.9 12.2 %copy-start.40 = (bf16[128,128]{1,0:T(8,128)(2,1)S(1)}, bf16[128,128]{1,0:T(8,128)(2,1)}, u32[]{:S(2)}) copy-start(bf16[128,128]{1,0:T(8,128)(2,1)} %param.33) | copy-start | bytes 98308
  119.5 1.4 collective-permute-start.4
  121.0 9.4 %collective-permute-start.5 = (bf16[16,8192]{1,0:T(8,128)(2,1)S(1)}, bf16[16,8192]{1,0:T(8,128)(2,1)S(1)}, u32[]{:S(2)}, u32[]{:S(2)}) collective-permute-start(bf16[16,8192]{1,0:T(8,128)(2,1)S(1)} %pad_maximum_fusion), channel_id=1, source_target_pairs={{0,8},{8,0},{16,24},{24,16},{32,40},{40,32},{48,56},{56,48},{64,72... | collective-permute-start | bytes 786440 | tf_op jit(solution)/shard_map/ppermute | solution.py:14
  132.8 8.2 %copy-start.41 = (bf16[128,128]{1,0:T(8,128)(2,1)S(1)}, bf16[128,128]{1,0:T(8,128)(2,1)}, u32[]{:S(2)}) copy-start(bf16[128,128]{1,0:T(8,128)(2,1)} %param.33) | copy-start | bytes 98308
  132.9 8.0 %collective-permute-start.6 = (bf16[16,8192]{1,0:T(8,128)(2,1)S(1)}, bf16[16,8192]{1,0:T(8,128)(2,1)S(1)}, u32[]{:S(2)}, u32[]{:S(2)}) collective-permute-start(bf16[16,8192]{1,0:T(8,128)(2,1)S(1)} %pad_maximum_fusion.1), channel_id=1, source_target_pairs={{0,8},{8,0},{16,24},{24,16},{32,40},{40,32},{48,56},{56,48},{64,72... | collective-permute-start | bytes 786440 | tf_op jit(solution)/shard_map/ppermute | solution.py:14
  141.0 1.4 collective-permute-start.7
  148.9 3.7 copy-start.29
  287.5 66.6 %collective-permute-start.9 = (bf16[1,8,4096]{2,1,0:T(8,128)(2,1)}, bf16[1,8,4096]{2,1,0:T(8,128)(2,1)}, u32[]{:S(2)}, u32[]{:S(2)}) collective-permute-start(bf16[1,8,4096]{2,1,0:T(8,128)(2,1)} %fusion.53), channel_id=1, source_target_pairs={{0,8},{8,16},{16,24},{24,32},{32,40},{40,48},{48,56},{56,64},{64,7... | collective-permute-start | bytes 196616 | tf_op jit(solution)/shard_map/ppermute | solution.py:22
  291.5 57.7 %collective-permute-start.10 = (bf16[1,8,4096]{2,1,0:T(8,128)(2,1)}, bf16[1,8,4096]{2,1,0:T(8,128)(2,1)}, u32[]{:S(2)}, u32[]{:S(2)}) collective-permute-start(bf16[1,8,4096]{2,1,0:T(8,128)(2,1)} %fusion.54), channel_id=1, source_target_pairs={{1,0},{2,1},{3,2},{4,3},{5,4},{6,5},{7,6},{9,8},{10,9},{11,10},{12... | collective-permute-start | bytes 196616 | tf_op jit(solution)/shard_map/ppermute | solution.py:25
  293.4 50.8 %collective-permute-start.8 = (bf16[1,8,4096]{2,1,0:T(8,128)(2,1)}, bf16[1,8,4096]{2,1,0:T(8,128)(2,1)}, u32[]{:S(2)}, u32[]{:S(2)}) collective-permute-start(bf16[1,8,4096]{2,1,0:T(8,128)(2,1)} %fusion.52), channel_id=1, source_target_pairs={{8,0},{16,8},{24,16},{32,24},{40,32},{48,40},{56,48},{64,56},{72,6... | collective-permute-start | bytes 196616 | tf_op jit(solution)/shard_map/ppermute | solution.py:25
  294.7 44.6 %collective-permute-start.11 = (bf16[1,8,4096]{2,1,0:T(8,128)(2,1)}, bf16[1,8,4096]{2,1,0:T(8,128)(2,1)}, u32[]{:S(2)}, u32[]{:S(2)}) collective-permute-start(bf16[1,8,4096]{2,1,0:T(8,128)(2,1)} %fusion.55), channel_id=1, source_target_pairs={{0,1},{1,2},{2,3},{3,4},{4,5},{5,6},{6,7},{8,9},{9,10},{10,11},{11... | collective-permute-start | bytes 196616 | tf_op jit(solution)/shard_map/ppermute | solution.py:22
  314.3 6.5 %copy-start.17 = (f32[8,64,1,2,2,1,4,4]{1,7,6,5,4,3,2,0:T(4,128)S(1)}, f32[8,64,1,2,2,1,4,4]{1,7,6,5,4,3,2,0:T(4,128)}, u32[]{:S(2)}) copy-start(f32[8,64,1,2,2,1,4,4]{1,7,6,5,4,3,2,0:T(4,128)} %copy.165) | copy-start | bytes 393220
  314.3 6.7 %copy-start.19 = (f32[8,64,1,2,2,1,4,4]{1,7,6,5,4,3,2,0:T(4,128)S(1)}, f32[8,64,1,2,2,1,4,4]{1,7,6,5,4,3,2,0:T(4,128)}, u32[]{:S(2)}) copy-start(f32[8,64,1,2,2,1,4,4]{1,7,6,5,4,3,2,0:T(4,128)} %copy.169) | copy-start | bytes 393220
  314.3 6.8 %copy-start.16 = (f32[8,64,2,1,2,4,1,4]{1,7,6,5,4,3,2,0:T(4,128)S(1)}, f32[8,64,2,1,2,4,1,4]{1,7,6,5,4,3,2,0:T(4,128)}, u32[]{:S(2)}) copy-start(f32[8,64,2,1,2,4,1,4]{1,7,6,5,4,3,2,0:T(4,128)} %copy.173) | copy-start | bytes 393220
  339.0 218.4 %all-reduce.13.cloned.1.call-start = ((), (), s32[]{:S(2)}) async-start(), calls=%async_computation.1 | async-start | bytes 917504 | tf_op jit(solution)/shard_map/psum | solution.py:281
  359.4 134.4 %copy-start.31 = (pred[8]{0:T(512)(128)(4,1)S(1)}, pred[8]{0:T(512)(128)(4,1)}, u32[]{:S(2)}) copy-start(pred[8]{0:T(512)(128)(4,1)} %copy-done.30) | copy-start | bytes 28
  493.8 68.4 %copy-start.1 = (bf16[128,512]{1,0:T(8,128)(2,1)S(1)}, bf16[128,512]{1,0:T(8,128)(2,1)}, u32[]{:S(2)}) copy-start(bf16[128,512]{1,0:T(8,128)(2,1)} %param.32) | copy-start | bytes 393220
  (26 other events, 53.8 us)
Sparse Core Ops, SparseCore 0:
  339.1 154.6 all-reduce.10
  496.3 61.0 all-reduce.12
